TPU v7x, 1024 devices: a whole 4x8x16 slice. The times are simulated.
1024 devices in a mesh: replica: 64 (over y_hi, z, core), shard: 16 (over x, y_lo).
Axes of the slice: x: 4, y: 8 (y_hi: 2, y_lo: 4; y = y_hi * 4 + y_lo), z: 16, core: 2. Of those that a mesh axis runs over, the one named last changes fastest.
Arguments:
- dec_grad: bfloat16 [1024, 16, 8192], P(('replica', 'shard')), may hold values from -0.25 to 0.25
- dec_master: float32 [16, 8192], P('shard'), may hold values from -6 to 6
- dec_moment: float32 [16, 8192], P('shard'), may hold values from -2 to 2
- dec_second: float32 [16, 8192], P('shard'), may hold values from 0.01 to 1
- vis_grad: bfloat16 [1024, 1280, 128], P(('replica', 'shard')), may hold values from -0.75 to 0.75
- vis_owner: int32 [1280], replicated, may hold values from 0 to 15, as said below
- vis_master: float32 [2560, 128], P('shard'), may hold values from -6 to 6
- vis_moment: float32 [2560, 128], P('shard'), may hold values from -2 to 2
- vis_second: float32 [2560, 128], P('shard'), may hold values from 0.01 to 1
- step_count: int32 [1], replicated, may hold values from 1 to 4096
Outputs:
- dec_master_new: float32 [16, 8192], P('shard')
- dec_moment_new: float32 [16, 8192], P('shard')
- dec_second_new: float32 [16, 8192], P('shard')
- dec_weight: bfloat16 [16, 8192], replicated
- vis_master_new: float32 [2560, 128], P('shard')
- vis_moment_new: float32 [2560, 128], P('shard')
- vis_second_new: float32 [2560, 128], P('shard')
- vis_weight: bfloat16 [1280, 128], replicated
Inputs may be any that keep to these rules, and one draw needn't show every extreme that they name: `vis_owner`: within each aligned range of 80 blocks, no owner receives more than 10 blocks; one owner, drawn afresh, receives exactly 10 blocks from every range and so 160 blocks in all.
All inputs are finite; a program needn't handle non-finite values.
Results may differ from a plain program's by a relative error of at most 0.001.
Values may be sent and summed in bfloat16 or wider, within the bound.
A program may use at most 32 MiB of HBM per device.

v0:
```python
import jax
import jax.numpy as jnp
from jax import lax
from jax.sharding import PartitionSpec as P

beta_one = 0.9
beta_two = 0.999
learn_rate = 0.02
weight_decay = 0.1
epsilon = 1e-08


def place_blocks(owner_map, range_size, per_source, owners):
    grouped = owner_map.reshape(-1, range_size)
    onehot = (grouped[:, :, None] == jnp.arange(owners, dtype=jnp.int32)[None, None, :]).astype(
        jnp.int32
    )
    position = jnp.sum((jnp.cumsum(onehot, axis=1) - onehot) * onehot, axis=2)
    source = jnp.arange(grouped.shape[0], dtype=jnp.int32)[:, None]
    return (grouped * (owners * per_source) + source * per_source + position).reshape(-1)


def adamw(gradient, moment, second, master, step_count):
    step_float = step_count[0].astype(jnp.float32)
    fix_one = 1.0 - jnp.power(beta_one, step_float)
    fix_two = 1.0 - jnp.power(beta_two, step_float)
    moment = beta_one * moment + (1.0 - beta_one) * gradient
    second = beta_two * second + (1.0 - beta_two) * gradient * gradient
    master = master - learn_rate * (
        moment / fix_one / (jnp.sqrt(second / fix_two) + epsilon) + weight_decay * master
    )
    return (moment, second, master)


def body(
    dec_grad,
    dec_master,
    dec_moment,
    dec_second,
    vis_grad,
    vis_owner,
    vis_master,
    vis_moment,
    vis_second,
    step_count,
):
    shards = lax.axis_size("shard")
    block_width = vis_grad.shape[2]
    range_size = vis_grad.shape[1] // shards
    per_source = 2 * range_size // shards
    capacity = shards * per_source
    row_of = place_blocks(vis_owner, range_size, per_source, shards)
    dec_terms = dec_grad[0]
    vis_terms = (
        jnp.zeros((shards * capacity, block_width), jnp.bfloat16).at[row_of].set(vis_grad[0])
    )
    dec_part, vis_part = (
        lax.psum_scatter(dec_terms.astype(jnp.float32), "shard", scatter_dimension=0, tiled=True),
        lax.psum_scatter(vis_terms.astype(jnp.float32), "shard", scatter_dimension=0, tiled=True),
    )
    dec_total, vis_reduced = lax.psum((dec_part, vis_part), "replica")
    dec_moment_new, dec_second_new, dec_master_new = adamw(
        dec_total, dec_moment, dec_second, dec_master, step_count
    )
    vis_moment_new, vis_second_new, vis_master_new = adamw(
        vis_reduced, vis_moment, vis_second, vis_master, step_count
    )
    dec_weight, vis_gathered = (
        lax.all_gather(dec_master_new.astype(jnp.bfloat16), "shard", axis=0, tiled=True),
        lax.all_gather(vis_master_new.astype(jnp.bfloat16), "shard", axis=0, tiled=True),
    )
    vis_weight = vis_gathered[row_of]
    return (
        dec_master_new,
        dec_moment_new,
        dec_second_new,
        dec_weight,
        vis_master_new,
        vis_moment_new,
        vis_second_new,
        vis_weight,
    )


def solution(mesh):
    in_specs = (
        P(("replica", "shard"), None, None),
        P("shard", None),
        P("shard", None),
        P("shard", None),
        P(("replica", "shard"), None, None),
        P(),
        P("shard", None),
        P("shard", None),
        P("shard", None),
        P(),
    )
    out_specs = (
        P("shard", None),
        P("shard", None),
        P("shard", None),
        P(),
        P("shard", None),
        P("shard", None),
        P("shard", None),
        P(),
    )
    return jax.shard_map(body, mesh=mesh, in_specs=in_specs, out_specs=out_specs, check_vma=False)
```

profile of v0, /device:TPU:1, one launch (start us, length us, event | category | flops | bytes accessed | tf_op | source)
XLA Modules:
  0.0 1173.4 jit_solution(18095245793052837848)
XLA Ops:
  7.2 0.0 all-reduce.6.cloned.1.call-start
  7.2 1.8 bitcast_convert_fusion
  9.1 0.0 reduce-scatter.2.cloned.1.call-start
  9.2 0.1 eq.15
  9.2 0.1 copy.20
  9.3 1.8 select_reduce_fusion
  11.1 0.1 copy.21
  11.2 0.1 reduce_sum.12
  11.3 0.1 add.62
  11.3 0.1 add.63
  11.4 6.6 scatter_custom_fusion
  18.1 1.1 convert_element_type.28
  19.2 0.0 all-reduce.4.cloned.1.call-start
  20.1 1.3 dynamic-slice
  21.3 166.7 %all-reduce.6.cloned.1.call-done = f32[16,8192]{1,0:T(8,128)} async-done(((f32[16,8192]{1,0:T(8,128)}), f32[16,8192]{1,0:T(8,128)}) %all-reduce.6.cloned.1.call-update) | async-done | bytes 524304
  188.1 1.6 constant_dynamic-slice_fusion
  189.7 337.8 %psum.14 = f32[1,8192]{1,0:T(1,128)S(1)} all-reduce(f32[1,8192]{1,0:T(1,128)S(1)} %constant_dynamic-slice_fusion), channel_id=1, replica_groups=mesh['replica'=64,'shard'=16] {'replica'}, use_global_device_ids=true, to_apply=%region_1.2 | all-reduce | flops 8192 | bytes 65536 | tf_op jit(solution)/shard_map/psum | solution.py:61
  527.5 0.9 convert_bitcast_fusion
  528.4 38.3 %all-gather = bf16[16,1,8192]{2,1,0:T(2,128)(2,1)S(1)} all-gather(bf16[1,1,8192]{2,1,0:T(2,128)(2,1)S(1)} %get-tuple-element.12), channel_id=1, replica_groups=mesh['replica'=64,'shard'=16] {'shard'}, dimensions={0}, use_global_device_ids=true | all-gather | bytes 278528 | tf_op jit(solution)/shard_map/all_gather | solution.py:69
  566.6 1.0 copy.24
  567.6 554.9 %all-reduce.4.cloned.1.call-done = f32[160,128]{1,0:T(8,128)} async-done(((f32[160,128]{1,0:T(8,128)}), f32[160,128]{1,0:T(8,128)}) %all-reduce.4.cloned.1.call-update) | async-done | bytes 81936 | tf_op jit(solution)/shard_map/psum | solution.py:61
  1122.5 1.6 fusion.10
  1124.1 39.2 %all_gather.7 = bf16[2560,128]{1,0:T(8,128)(2,1)S(1)} all-gather(bf16[160,128]{1,0:T(8,128)(2,1)S(1)} %get-tuple-element.8), channel_id=1, replica_groups=mesh['replica'=64,'shard'=16] {'shard'}, dimensions={0}, use_global_device_ids=true | all-gather | bytes 696320 | tf_op jit(solution)/shard_map/all_gather | solution.py:70
  1163.3 3.5 gather_fusion
  (23 shorter events, 0.1 us)
Async XLA Ops:
  7.2 4.3 copy-start
  7.2 2.0 copy-start.4
  7.2 180.9 %all-reduce.6.cloned.1.call-start = ((), (), s32[]{:S(2)}) async-start(), calls=%async_computation.3 | async-start | bytes 1048576
  9.1 519.3 %reduce-scatter.2.cloned.1.call-start = ((), (), s32[]{:S(2)}) async-start(), calls=%async_computation.1 | async-start | bytes 1392640 | tf_op jit(solution)/shard_map/reduce_scatter | solution.py:59
  18.0 509.5 %copy-start.5 = (f32[1,8192]{1,0:T(1,128)S(1)}, f32[1,8192]{1,0:T(1,128)}, u32[]{:S(2)}) copy-start(f32[1,8192]{1,0:T(1,128)} %param.11) | copy-start | bytes 98308
  18.0 509.5 %copy-start.6 = (f32[1,8192]{1,0:T(1,128)S(1)}, f32[1,8192]{1,0:T(1,128)}, u32[]{:S(2)}) copy-start(f32[1,8192]{1,0:T(1,128)} %param.13) | copy-start | bytes 98308
  18.0 509.5 %copy-start.7 = (f32[1,8192]{1,0:T(1,128)S(1)}, f32[1,8192]{1,0:T(1,128)}, u32[]{:S(2)}) copy-start(f32[1,8192]{1,0:T(1,128)} %param.12) | copy-start | bytes 98308
  19.2 1103.3 %copy-start.1 = (f32[160,128]{1,0:T(8,128)S(1)}, f32[160,128]{1,0:T(8,128)}, u32[]{:S(2)}) copy-start(f32[160,128]{1,0:T(8,128)} %param.16) | copy-start | bytes 245764
  19.2 1103.3 %copy-start.2 = (f32[160,128]{1,0:T(8,128)S(1)}, f32[160,128]{1,0:T(8,128)}, u32[]{:S(2)}) copy-start(f32[160,128]{1,0:T(8,128)} %param.18) | copy-start | bytes 245764
  19.2 1103.3 %copy-start.3 = (f32[160,128]{1,0:T(8,128)S(1)}, f32[160,128]{1,0:T(8,128)}, u32[]{:S(2)}) copy-start(f32[160,128]{1,0:T(8,128)} %param.17) | copy-start | bytes 245764
  19.2 1103.3 %all-reduce.4.cloned.1.call-start = ((), (), s32[]{:S(2)}) async-start(), calls=%async_computation.2 | async-start | bytes 163840 | tf_op jit(solution)/shard_map/psum | solution.py:61
Sparse Core Ops, SparseCore 0:
  11.5 176.5 all-reduce.5
  191.5 95.0 reduce-scatter.1
  528.5 593.9 all-reduce.3
where the time goes:
time: 1180 us; the launch traced here: 1170 us
  waiting for transfers between devices  722 us (61%)
  blocking collectives  415 us (35%)
  between operations  14.6 us (1%)
  local copies, waits for them, and re-layouts  14.5 us (1%)
    psum x1, waiting for transfers between devices, body(): dec_total, vis_reduced = lax.psum((dec_part, vis_part), 'replica')  555 us
    psum x1, blocking collectives, body(): dec_total, vis_reduced = lax.psum((dec_part, vis_part), 'replica')  338 us
    unnamed x4, waiting for transfers between devices  167 us
    all_gather x1, blocking collectives, body(): lax.all_gather(vis_master_new.astype(jnp.bfloat16), 'shard', axis=0, tile...  39.2 us
    all_gather x1, blocking collectives, body(): lax.all_gather(dec_master_new.astype(jnp.bfloat16), 'shard', axis=0, tile...  38.3 us
  transfers between devices with their start and end apart: 3, of which 2 were waited for; matrix products, arithmetic and copies ran while one was open for 1% of the time, Pallas kernels for 0%

commit v1 on v0

v1 whole, which is shorter than its diff:
```python
import math

import jax
import jax.numpy as jnp
from jax import lax
from jax.experimental import pallas as pl
from jax.experimental.pallas import tpu as pltpu
from jax.sharding import PartitionSpec as P

beta_one = 0.9
beta_two = 0.999
learn_rate = 0.02
weight_decay = 0.1
epsilon = 1e-08

MESH = pl.DeviceIdType.MESH
F32 = jnp.float32
BF16 = jnp.bfloat16
HIGH = lax.Precision.HIGHEST

NX, NY, NZ = 4, 8, 16
Q = 4
ROWS = 80
DEC = 64
PAD = 96
PART = PAD // 4
SLOT = 16
USED = 10
CAP = 160


def adamw(g, m, v, p, inv_one, inv_two):
    m = beta_one * m + (1.0 - beta_one) * g
    v = beta_two * v + (1.0 - beta_two) * g * g
    p = p - learn_rate * (m * inv_one / (jnp.sqrt(v * inv_two) + epsilon) + weight_decay * p)
    return m, v, p


def kernel(
    step_ref,
    own_ref,
    dec_grad,
    vis_grad,
    dec_p,
    dec_m,
    dec_v,
    vis_p,
    vis_m,
    vis_v,
    o_dp,
    o_dm,
    o_dv,
    o_dw,
    o_vp,
    o_vm,
    o_vv,
    o_vw,
    a_dec,
    b_dec,
    a_vis,
    b_vis,
    s_dec,
    s_vis,
    acc,
    ry,
    ay,
    rx,
    ax,
    rz,
    az,
    ryh,
    ah,
    rzh,
    tz,
    g4,
    gdec,
    wall,
    st,
    stm,
    stx,
    gx,
    gm,
    gr,
    n_dec,
    n_vis,
    wide,
    dw,
    lsem,
    ssem,
    rsem,
):
    rep, sh = lax.axis_index("replica"), lax.axis_index("shard")
    core = lax.rem(rep, 2)
    z = lax.rem(rep // 2, NZ)
    yl = lax.rem(sh, Q)
    y = (rep // (2 * NZ)) * Q + yl
    x = sh // Q
    zq = lax.rem(z, 4)

    def dev(dx=0, dy=0, dz=0, dc=0):
        xx = lax.rem(x + dx + NX, NX)
        yy = lax.rem(y + dy + NY, NY)
        zz = lax.rem(z + dz + NZ, NZ)
        cc = lax.rem(core + dc, 2)
        return ((yy // Q) * NZ + zz) * 2 + cc, xx * Q + lax.rem(yy, Q)

    def at4(i, d):
        return lax.rem(i + d + 4, 4)

    used = [0]

    def remote(src, dst, target):
        k = used[0]
        used[0] += 1
        return pltpu.make_async_remote_copy(
            src_ref=src,
            dst_ref=dst,
            send_sem=ssem.at[k],
            recv_sem=rsem.at[k],
            device_id=target,
            device_id_type=MESH,
        )

    locals_used = [0]

    def local(src, dst):
        k = locals_used[0]
        locals_used[0] += 1
        return pltpu.make_async_copy(src, dst, lsem.at[k])

    def go(copies):
        for c in copies:
            c.start()

    def done(copies):
        for c in copies:
            c.wait()

    is_dec, is_vis = core == 0, core == 1

    load_dec = local(dec_grad.at[0], a_dec)
    load_vis = local(vis_grad.at[0], a_vis)
    load_state = [
        local(src, dst)
        for src, dst in (
            (dec_p, s_dec.at[0]),
            (dec_m, s_dec.at[1]),
            (dec_v, s_dec.at[2]),
            (vis_p, s_vis.at[0]),
            (vis_m, s_vis.at[1]),
            (vis_v, s_vis.at[2]),
        )
    ]

    @pl.when(is_dec)
    def _():
        load_dec.start()

    @pl.when(is_vis)
    def _():
        load_vis.start()

    go(load_state)

    friends = [dev(dc=1)]
    friends += [dev(dx=d) for d in (1, -1, 2)]
    friends += [dev(dy=d) for d in (1, -1, 2, -2, 4)]
    friends += [dev(dz=d) for d in (1, -1, 2, -2, 4, -4, 8)]
    barrier = pltpu.get_barrier_semaphore()
    for friend in friends:
        pl.semaphore_signal(barrier, inc=1, device_id=friend, device_id_type=MESH)
    pl.semaphore_wait(barrier, len(friends))

    send_vis = remote(vis_grad.at[0], b_vis, dev(dc=1))
    send_dec = remote(dec_grad.at[0], b_dec, dev(dc=1))

    @pl.when(is_dec)
    def _():
        send_vis.start()
        load_dec.wait()
        send_dec.wait_recv()

        @pl.loop(0, DEC)
        def _(j):
            at = pl.multiple_of(j * 128, 128)
            block = a_dec[:, pl.ds(at, 128)].astype(F32) + b_dec[:, pl.ds(at, 128)].astype(F32)
            acc.reshape(16 * ROWS, 128)[pl.ds(j, 16, stride=ROWS), :] = block

        for i in range(16):
            acc[i // 4, i % 4, DEC:ROWS, :] = jnp.zeros((ROWS - DEC, 128), F32)
        send_vis.wait_send()

    @pl.when(is_vis)
    def _():
        send_dec.start()
        load_vis.wait()
        send_vis.wait_recv()

        for i in range(16):
            part = pl.ds(i * ROWS, ROWS)
            acc[i // 4, i % 4] = a_vis[part, :].astype(F32) + b_vis[part, :].astype(F32)
        send_dec.wait_send()

    q1, q2, q3 = at4(yl, 1), at4(yl, 2), at4(yl, 3)
    lo, hi = pl.ds(0, 2), pl.ds(2, 2)
    copies = [
        remote(acc.at[lo, q2], ry.at[2, lo], dev(dy=2)),
        remote(acc.at[hi, q2], ry.at[2, hi], dev(dy=-2)),
        remote(acc.at[:, q1], ry.at[0], dev(dy=1)),
        remote(acc.at[:, q3], ry.at[1], dev(dy=-1)),
    ]
    go(copies)
    done(copies)
    for i in range(NX):
        ay[i] = (acc[i, yl] + ry[0, i]) + (ry[1, i] + ry[2, i])

    copies = [
        remote(ay.at[at4(x, 2)], rx.at[2], dev(dx=2)),
        remote(ay.at[at4(x, 1)], rx.at[0], dev(dx=1)),
        remote(ay.at[at4(x, 3)], rx.at[1], dev(dx=-1)),
    ]
    go(copies)
    done(copies)
    ax[0:ROWS, :] = (ay[x] + rx[0]) + (rx[1] + rx[2])
    ax[ROWS:PAD, :] = jnp.zeros((PAD - ROWS, 128), F32)

    def part_of(i):
        return pl.ds(pl.multiple_of(i * PART, 8), PART)

    copies = [
        remote(ax.at[part_of(at4(zq, 2))], rz.at[2], dev(dz=2)),
        remote(ax.at[part_of(at4(zq, 1))], rz.at[0], dev(dz=1)),
        remote(ax.at[part_of(at4(zq, 3))], rz.at[1], dev(dz=-1)),
    ]
    go(copies)

    done(load_state)
    for i in range(16):
        for k in range(3):
            st[i, k * SLOT : k * SLOT + SLOT, :] = jnp.zeros((SLOT, 128), F32)
            st[i, k * SLOT : k * SLOT + USED, :] = s_vis[k, i * USED : i * USED + USED, :]

    def along_x(src, dst):
        return [
            remote(src.at[pl.ds(at4(x, d) * 4, 4)], dst.at[x], dev(dx=e))
            for d, e in ((2, 2), (1, 1), (3, -1))
        ]

    def along_y(src, dst):
        return [
            remote(src.at[:, at4(yl, d)], dst.at[:, yl], dev(dy=e))
            for d, e in ((2, 2), (1, 1), (3, -1))
        ]

    st_x = along_x(st, stm)
    st_y = along_y(stm, stx)
    back = [at4(x, d) for d in (-2, -1, 1)]

    @pl.when(is_vis)
    def _():
        go(st_x)
        stm[x] = st[pl.ds(x * 4, 4)]

    done(copies)
    az[...] = (ax[part_of(zq), :] + rz[0]) + (rz[1] + rz[2])

    far = remote(az, ryh, dev(dy=4))
    far.start()

    @pl.when(is_vis)
    def _():
        done(st_x)

    far.wait()
    ah[...] = az[...] + ryh[...]
    copies = [
        remote(ah, rzh.at[2], dev(dz=8)),
        remote(ah, rzh.at[0], dev(dz=4)),
        remote(ah, rzh.at[1], dev(dz=-4)),
    ]
    go(copies)

    @pl.when(is_vis)
    def _():
        go(st_y)
        stx[:, yl] = stm[:, yl]

    t = jnp.full((1, 128), step_ref[0].astype(F32), F32)
    inv_one = 1.0 / (1.0 - jnp.exp(t * math.log(beta_one)))
    inv_two = 1.0 / (1.0 - jnp.exp(t * math.log(beta_two)))

    own = own_ref[pl.ds(sh, 1), :]
    one_hot = (lax.broadcasted_iota(jnp.int32, (16, ROWS), 0) == own).astype(F32)
    before = (
        lax.broadcasted_iota(jnp.int32, (ROWS, ROWS), 0)
        < lax.broadcasted_iota(jnp.int32, (ROWS, ROWS), 1)
    ).astype(F32)
    count = jnp.dot(one_hot, before, preferred_element_type=F32)
    position = jnp.sum(one_hot * count, axis=0, keepdims=True)
    key = own * SLOT + position.astype(jnp.int32)
    pick = (lax.broadcasted_iota(jnp.int32, (16 * SLOT, ROWS), 0) == key).astype(F32)

    def blocks_of(k):
        rows = stx[:, :, k * SLOT : k * SLOT + SLOT, :].reshape(16 * SLOT, 128)
        return lax.dot_general(
            pick, rows, (((0,), (0,)), ((), ())), precision=HIGH, preferred_element_type=F32
        )

    @pl.when(is_vis)
    def _():
        done(st_y)
        for k in range(3):
            n_vis[k, 0:ROWS, :] = blocks_of(k)

    done(copies)
    tz[...] = (ah[...] + rzh[2]) + (rzh[0] + rzh[1])

    copies = [
        remote(tz, g4.at[zq], dev(dz=2)),
        remote(tz, g4.at[zq], dev(dz=1)),
        remote(tz, g4.at[zq], dev(dz=-1)),
    ]
    go(copies)
    g4[zq] = tz[...]
    done(copies)

    g_x = along_x(gx, gm)
    g_y = along_y(gm, gr)
    dec_over = remote(gdec, gdec, dev(dc=1))
    vis_over = remote(gr, gr, dev(dc=1))

    @pl.when(is_dec)
    def _():
        g = g4[...].reshape(PAD, 128)[0:DEC]
        gdec[...] = g
        dec_over.start()
        _, _, p = adamw(g, s_dec[1], s_dec[2], s_dec[0], inv_one, inv_two)
        wall[x, yl, 0:DEC, :] = p.astype(BF16)
        wall[x, yl, DEC:ROWS, :] = jnp.zeros((ROWS - DEC, 128), BF16)

    @pl.when(is_vis)
    def _():
        g = g4[...].reshape(PAD, 128)[0:ROWS]
        _, _, p = adamw(
            g, n_vis[1, 0:ROWS, :], n_vis[2, 0:ROWS, :], n_vis[0, 0:ROWS, :], inv_one, inv_two
        )
        wall[x, yl] = p.astype(BF16)

    w_x = [remote(wall.at[x, yl], wall.at[x, yl], dev(dx=d)) for d in (2, 1, -1)]
    go(w_x)

    @pl.when(is_vis)
    def _():
        g = g4[...].reshape(PAD, 128)[0:ROWS]
        rows = jnp.dot(pick, g, precision=HIGH, preferred_element_type=F32)
        gx[...] = rows.reshape(16, SLOT, 128)
        go(g_x)
        gm[x] = gx[pl.ds(x * 4, 4)]

    done(w_x)
    w_y = [
        remote(wall.at[lo, yl], wall.at[lo, yl], dev(dy=2)),
        remote(wall.at[hi, yl], wall.at[hi, yl], dev(dy=-2)),
        remote(wall.at[:, yl], wall.at[:, yl], dev(dy=1)),
        remote(wall.at[:, yl], wall.at[:, yl], dev(dy=-1)),
    ]
    go(w_y)

    outs_dec = [local(n_dec.at[k], o) for k, o in enumerate((o_dp, o_dm, o_dv))]
    outs_vis = [local(n_vis.at[k], o) for k, o in enumerate((o_vp, o_vm, o_vv))]

    @pl.when(is_vis)
    def _():
        done(g_x)
        go(g_y)
        gr[:, yl] = gm[:, yl]
        dec_over.wait_recv()

    m, v, p = adamw(gdec[...], s_dec[1], s_dec[2], s_dec[0], inv_one, inv_two)
    n_dec[0], n_dec[1], n_dec[2] = p, m, v
    go(outs_dec)

    @pl.when(is_vis)
    def _():
        done(g_y)
        vis_over.start()

    @pl.when(is_dec)
    def _():
        vis_over.wait_recv()

    for i in range(16):
        part = pl.ds(i * USED, USED)
        g = gr[i // 4, i % 4, 0:USED, :]
        m, v, p = adamw(
            g, s_vis[1, part, :], s_vis[2, part, :], s_vis[0, part, :], inv_one, inv_two
        )
        n_vis[0, part, :] = p
        n_vis[1, part, :] = m
        n_vis[2, part, :] = v
    go(outs_vis)
    done(w_y)

    out_vw, out_dw = local(wall.reshape(16 * ROWS, 128), o_vw), local(dw, o_dw)
    over_vw = remote(wall.reshape(16 * ROWS, 128), o_vw, dev(dc=1))
    over_dw = remote(dw, o_dw, dev(dc=1))

    @pl.when(is_vis)
    def _():
        over_vw.start()
        out_vw.start()
        over_dw.wait_recv()
        out_vw.wait()
        over_vw.wait_send()
        vis_over.wait_send()

    @pl.when(is_dec)
    def _():
        for i in range(16):
            wide[i * DEC : i * DEC + DEC, :] = wall[i // 4, i % 4, 0:DEC, :].astype(F32)

        @pl.loop(0, DEC)
        def _(j):
            at = pl.multiple_of(j * 128, 128)
            dw[:, pl.ds(at, 128)] = wide[pl.ds(j, 16, stride=DEC), :].astype(BF16)

        over_dw.start()
        out_dw.start()
        over_vw.wait_recv()
        out_dw.wait()
        over_dw.wait_send()
        dec_over.wait_send()

    done(outs_dec)
    done(outs_vis)


def body(
    dec_grad,
    dec_master,
    dec_moment,
    dec_second,
    vis_grad,
    vis_owner,
    vis_master,
    vis_moment,
    vis_second,
    step_count,
):
    anywhere = pl.BlockSpec(memory_space=pl.ANY)
    sds = jax.ShapeDtypeStruct
    vmem = pltpu.VMEM
    out_shape = [
        sds((DEC, 128), F32),
        sds((DEC, 128), F32),
        sds((DEC, 128), F32),
        sds((16, DEC * 128), BF16),
        sds((CAP, 128), F32),
        sds((CAP, 128), F32),
        sds((CAP, 128), F32),
        sds((16 * ROWS, 128), BF16),
    ]
    scratch = [
        vmem((16, DEC * 128), BF16),
        vmem((16, DEC * 128), BF16),
        vmem((16 * ROWS, 128), BF16),
        vmem((16 * ROWS, 128), BF16),
        vmem((3, DEC, 128), F32),
        vmem((3, CAP, 128), F32),
        vmem((4, 4, ROWS, 128), F32),
        vmem((3, 4, ROWS, 128), F32),
        vmem((4, ROWS, 128), F32),
        vmem((3, ROWS, 128), F32),
        vmem((PAD, 128), F32),
        vmem((3, PART, 128), F32),
        vmem((PART, 128), F32),
        vmem((PART, 128), F32),
        vmem((PART, 128), F32),
        vmem((3, PART, 128), F32),
        vmem((PART, 128), F32),
        vmem((4, PART, 128), F32),
        vmem((DEC, 128), F32),
        vmem((4, 4, ROWS, 128), BF16),
        vmem((16, 3 * SLOT, 128), F32),
        vmem((4, 4, 3 * SLOT, 128), F32),
        vmem((4, 4, 3 * SLOT, 128), F32),
        vmem((16, SLOT, 128), F32),
        vmem((4, 4, SLOT, 128), F32),
        vmem((4, 4, SLOT, 128), F32),
        vmem((3, DEC, 128), F32),
        vmem((3, CAP, 128), F32),
        vmem((16 * DEC, 128), F32),
        vmem((16, DEC * 128), BF16),
        pltpu.SemaphoreType.DMA((20,)),
        pltpu.SemaphoreType.DMA((64,)),
        pltpu.SemaphoreType.DMA((64,)),
    ]
    outs = pl.pallas_call(
        kernel,
        out_shape=out_shape,
        in_specs=[pl.BlockSpec(memory_space=pltpu.SMEM), pl.BlockSpec(memory_space=pltpu.VMEM)]
        + [anywhere] * 8,
        out_specs=[anywhere] * 8,
        scratch_shapes=scratch,
        compiler_params=pltpu.CompilerParams(collective_id=0, has_side_effects=True),
    )(
        step_count,
        vis_owner.reshape(16, ROWS),
        dec_grad,
        vis_grad,
        dec_master.reshape(DEC, 128),
        dec_moment.reshape(DEC, 128),
        dec_second.reshape(DEC, 128),
        vis_master,
        vis_moment,
        vis_second,
    )
    outs = list(outs)
    for i in range(3):
        outs[i] = outs[i].reshape(1, DEC * 128)
    return tuple(outs)


def solution(mesh):
    in_specs = (
        P(("replica", "shard"), None, None),
        P("shard", None),
        P("shard", None),
        P("shard", None),
        P(("replica", "shard"), None, None),
        P(),
        P("shard", None),
        P("shard", None),
        P("shard", None),
        P(),
    )
    out_specs = (
        P("shard", None),
        P("shard", None),
        P("shard", None),
        P(),
        P("shard", None),
        P("shard", None),
        P("shard", None),
        P(),
    )
    return jax.shard_map(body, mesh=mesh, in_specs=in_specs, out_specs=out_specs, check_vma=False)
```

time: 1180 us -> 82.6 us (0.07)
  waiting for transfers between devices: 722 us -> 0 us
  blocking collectives: 415 us -> 0 us
  Pallas kernels: 0 us -> 72.4 us
  between operations: 14.6 us -> 1.31 us
    psum x1 -> x0, waiting for transfers between devices: 555 us -> none  [body(): dec_total, vis_reduced = lax.psum((dec_part, vis_part), 'replica')]
    psum x1 -> x0, blocking collectives: 338 us -> none  [body(): dec_total, vis_reduced = lax.psum((dec_part, vis_part), 'replica')]
    unnamed x4 -> x0, waiting for transfers between devices: 167 us -> none
    all_gather x2 -> x0, blocking collectives: 77.4 us -> none  [the longest x1 39.2 us: body(): lax.all_gather(vis_master_new.astype(jnp.bfloat16), 'shard', axis=0, tile...]
    pallas_call x0 -> x1, Pallas kernels: none -> 72.4 us  [body(): pl.pallas_call(kernel, out_shape=out_shape, in_specs=[pl.BlockSpec(memory...]
  transfers between devices with their start and end apart: 3 -> 0, of which waited for: 2 -> 0; matrix products, arithmetic and copies ran while one was open for 1% -> 0% of each run, Pallas kernels for 0% -> 0%
where the time goes in v1:
time: 82.6 us; the launch traced here: 82.2 us
  Pallas kernels  72.4 us (88%)
  local copies, waits for them, and re-layouts  8.49 us (10%)
  between operations  1.31 us (2%)
    pallas_call x1, Pallas kernels, body(): pl.pallas_call(kernel, out_shape=out_shape, in_specs=[pl.BlockSpec(memory...  72.4 us
    unnamed x20, local copies, waits for them, and re-layouts  7.12 us

profile of v1, /device:TPU:1, one launch (start us, length us, event | category | flops | bytes accessed | tf_op | source)
XLA Modules:
  0.0 82.2 jit_solution(5301417309005995133)
XLA Ops:
  1.3 1.4 %reshape.37.own_ref = s32[16,80]{1,0:T(8,128)} reshape(s32[1280]{0:T(1024)} %param.15) | data formatting | bytes 10240 | tf_op jit(solution)/shard_map/reshape | solution.py:508
  2.7 72.4 %shard_map.161 = (f32[64,128]{1,0:T(8,128)}, f32[64,128]{1,0:T(8,128)}, f32[64,128]{1,0:T(8,128)}, bf16[16,8192]{1,0:T(8,128)(2,1)}, f32[160,128]{1,0:T(8,128)},...) custom-call(s32[1]{0:T(128)S(6)} %copy.26.step_ref, s32[16,80]{1,0:T(8,128)} %reshape.37.own_ref, ...), custom_call_target="tpu_custom_call" | custom-call | tf_op jit(solution)/shard_map/pallas_call | solution.py:498
  75.0 0.0 copy-start.5
  75.0 1.4 %copy.27 = f32[1,8192]{1,0:T(1,128)} copy(f32[1,8192]{1,0:T(1,128)} %bitcast.11) | data formatting | bytes 65536
  76.4 0.0 copy-done.5
  76.4 0.0 copy-start.4
  76.4 0.6 copy.28
  77.0 0.2 copy-done.4
  77.2 0.6 copy.29
  77.8 0.0 copy-start.3
  77.8 0.0 copy-start.2
  77.8 0.0 copy-start.1
  77.8 1.7 %copy.30 = bf16[16,8192]{1,0:T(8,128)(2,1)} copy(bf16[16,8192]{1,0:T(8,128)(2,1)} %get-tuple-element.35) | data formatting | bytes 524288
  79.5 0.0 copy-done.3
  79.5 0.0 copy-start
  79.5 0.6 copy.31
  80.2 0.0 copy-done.2
  80.2 0.6 copy.32
  80.8 0.0 copy-done.1
  80.8 0.6 copy.33
  81.5 0.0 copy-done
  81.5 0.7 copy.34
Async XLA Ops:
  75.0 1.4 %copy-start.5 = (f32[64,128]{1,0:T(8,128)S(1)}, f32[64,128]{1,0:T(8,128)}, u32[]{:S(2)}) copy-start(f32[64,128]{1,0:T(8,128)} %get-tuple-element.17) | copy-start | bytes 98308
  76.4 0.8 copy-start.4
  77.8 1.7 %copy-start.3 = (f32[160,128]{1,0:T(8,128)S(1)}, f32[160,128]{1,0:T(8,128)}, u32[]{:S(2)}) copy-start(f32[160,128]{1,0:T(8,128)} %get-tuple-element.36) | copy-start | bytes 245764
  77.8 2.4 %copy-start.2 = (f32[160,128]{1,0:T(8,128)S(1)}, f32[160,128]{1,0:T(8,128)}, u32[]{:S(2)}) copy-start(f32[160,128]{1,0:T(8,128)} %get-tuple-element.37) | copy-start | bytes 245764
  77.8 3.0 %copy-start.1 = (f32[160,128]{1,0:T(8,128)S(1)}, f32[160,128]{1,0:T(8,128)}, u32[]{:S(2)}) copy-start(f32[160,128]{1,0:T(8,128)} %get-tuple-element.38) | copy-start | bytes 245764
  79.5 1.9 %copy-start = (bf16[1280,128]{1,0:T(8,128)(2,1)S(1)}, bf16[1280,128]{1,0:T(8,128)(2,1)}, u32[]{:S(2)}) copy-start(bf16[1280,128]{1,0:T(8,128)(2,1)} %get-tuple-element.39) | copy-start | bytes 983044

commit v2 on v1

--- a/solution.py
+++ b/solution.py
@@ -1,3 +1,4 @@
+import itertools
 import math
 
 import jax
@@ -23,6 +24,8 @@
 ROWS = 80
 DEC = 64
 PAD = 96
+HALF = ROWS // 2
+CUT = 48
 PART = PAD // 4
 SLOT = 16
 USED = 10
@@ -47,14 +50,10 @@
     vis_p,
     vis_m,
     vis_v,
-    o_dp,
-    o_dm,
-    o_dv,
-    o_dw,
-    o_vp,
-    o_vm,
-    o_vv,
-    o_vw,
+    n_dec,
+    n_vis,
+    w_dec,
+    w_vis,
     a_dec,
     b_dec,
     a_vis,
@@ -65,6 +64,9 @@
     ry,
     ay,
     rx,
+    ak,
+    rx2,
+    ry2,
     ax,
     rz,
     az,
@@ -81,10 +83,7 @@
     gx,
     gm,
     gr,
-    n_dec,
-    n_vis,
-    wide,
-    dw,
+    owner,
     lsem,
     ssem,
     rsem,
@@ -140,6 +139,7 @@
 
     load_dec = local(dec_grad.at[0], a_dec)
     load_vis = local(vis_grad.at[0], a_vis)
+    load_maps = [local(own_ref, owner)]
     load_state = [
         local(src, dst)
         for src, dst in (
@@ -160,6 +160,7 @@
     def _():
         load_vis.start()
 
+    go(load_maps)
     go(load_state)
 
     friends = [dev(dc=1)]
@@ -202,26 +203,46 @@
         send_dec.wait_send()
 
     q1, q2, q3 = at4(yl, 1), at4(yl, 2), at4(yl, 3)
+    x1, x2, x3 = at4(x, 1), at4(x, 2), at4(x, 3)
     lo, hi = pl.ds(0, 2), pl.ds(2, 2)
-    copies = [
-        remote(acc.at[lo, q2], ry.at[2, lo], dev(dy=2)),
-        remote(acc.at[hi, q2], ry.at[2, hi], dev(dy=-2)),
-        remote(acc.at[:, q1], ry.at[0], dev(dy=1)),
-        remote(acc.at[:, q3], ry.at[1], dev(dy=-1)),
-    ]
-    go(copies)
-    done(copies)
+    one, two = pl.ds(0, HALF), pl.ds(HALF, HALF)
+    first_y = [
+        remote(acc.at[lo, q2, one], ry.at[2, lo], dev(dy=2)),
+        remote(acc.at[hi, q2, one], ry.at[2, hi], dev(dy=-2)),
+        remote(acc.at[:, q1, one], ry.at[0], dev(dy=1)),
+        remote(acc.at[:, q3, one], ry.at[1], dev(dy=-1)),
+    ]
+    first_x = [
+        remote(acc.at[x2, :, two], rx.at[2], dev(dx=2)),
+        remote(acc.at[x1, :, two], rx.at[0], dev(dx=1)),
+        remote(acc.at[x3, :, two], rx.at[1], dev(dx=-1)),
+    ]
+    for a, b in itertools.zip_longest(first_y, first_x):
+        a.start()
+        if b is not None:
+            b.start()
+    second_x = [
+        remote(ay.at[x2], rx2.at[2], dev(dx=2)),
+        remote(ay.at[x1], rx2.at[0], dev(dx=1)),
+        remote(ay.at[x3], rx2.at[1], dev(dx=-1)),
+    ]
+    second_y = [
+        remote(ak.at[q2], ry2.at[2], dev(dy=2)),
+        remote(ak.at[q1], ry2.at[0], dev(dy=1)),
+        remote(ak.at[q3], ry2.at[1], dev(dy=-1)),
+    ]
+    done(first_y)
     for i in range(NX):
-        ay[i] = (acc[i, yl] + ry[0, i]) + (ry[1, i] + ry[2, i])
-
-    copies = [
-        remote(ay.at[at4(x, 2)], rx.at[2], dev(dx=2)),
-        remote(ay.at[at4(x, 1)], rx.at[0], dev(dx=1)),
-        remote(ay.at[at4(x, 3)], rx.at[1], dev(dx=-1)),
-    ]
-    go(copies)
-    done(copies)
-    ax[0:ROWS, :] = (ay[x] + rx[0]) + (rx[1] + rx[2])
+        ay[i] = (acc[i, yl, one, :] + ry[0, i]) + (ry[1, i] + ry[2, i])
+    go(second_x)
+    done(first_x)
+    for i in range(Q):
+        ak[i] = (acc[x, i, two, :] + rx[0, i]) + (rx[1, i] + rx[2, i])
+    go(second_y)
+    done(second_x)
+    ax[0:HALF, :] = (ay[x] + rx2[0]) + (rx2[1] + rx2[2])
+    done(second_y)
+    ax[HALF:ROWS, :] = (ak[yl] + ry2[0]) + (ry2[1] + ry2[2])
     ax[ROWS:PAD, :] = jnp.zeros((PAD - ROWS, 128), F32)
 
     def part_of(i):
@@ -285,11 +306,18 @@
         go(st_y)
         stx[:, yl] = stm[:, yl]
 
+    done(load_maps)
     t = jnp.full((1, 128), step_ref[0].astype(F32), F32)
     inv_one = 1.0 / (1.0 - jnp.exp(t * math.log(beta_one)))
     inv_two = 1.0 / (1.0 - jnp.exp(t * math.log(beta_two)))
 
-    own = own_ref[pl.ds(sh, 1), :]
+    lane = lax.broadcasted_iota(jnp.int32, (1, ROWS), 1)
+    own = lax.fori_loop(
+        0,
+        ROWS,
+        lambda i, v: jnp.where(lane == i, owner[sh * ROWS + i], v),
+        jnp.zeros((1, ROWS), jnp.int32),
+    )
     one_hot = (lax.broadcasted_iota(jnp.int32, (16, ROWS), 0) == own).astype(F32)
     before = (
         lax.broadcasted_iota(jnp.int32, (ROWS, ROWS), 0)
@@ -346,8 +374,15 @@
         )
         wall[x, yl] = p.astype(BF16)
 
-    w_x = [remote(wall.at[x, yl], wall.at[x, yl], dev(dx=d)) for d in (2, 1, -1)]
+    up, down = pl.ds(0, CUT), pl.ds(CUT, ROWS - CUT)
+
+    def weights(view, device):
+        return remote(view, view, device)
+
+    w_x = [weights(wall.at[x, yl, up], dev(dx=d)) for d in (2, 1, -1)]
+    w_y = [weights(wall.at[x, yl, down], dev(dy=d)) for d in (2, 1, -1)]
     go(w_x)
+    go(w_y)
 
     @pl.when(is_vis)
     def _():
@@ -357,17 +392,17 @@
         go(g_x)
         gm[x] = gx[pl.ds(x * 4, 4)]
 
+    w_xy = [
+        weights(wall.at[lo, yl, up], dev(dy=2)),
+        weights(wall.at[hi, yl, up], dev(dy=-2)),
+        weights(wall.at[:, yl, up], dev(dy=1)),
+        weights(wall.at[:, yl, up], dev(dy=-1)),
+    ]
+    w_yx = [weights(wall.at[x, :, down], dev(dx=d)) for d in (2, 1, -1)]
     done(w_x)
-    w_y = [
-        remote(wall.at[lo, yl], wall.at[lo, yl], dev(dy=2)),
-        remote(wall.at[hi, yl], wall.at[hi, yl], dev(dy=-2)),
-        remote(wall.at[:, yl], wall.at[:, yl], dev(dy=1)),
-        remote(wall.at[:, yl], wall.at[:, yl], dev(dy=-1)),
-    ]
-    go(w_y)
-
-    outs_dec = [local(n_dec.at[k], o) for k, o in enumerate((o_dp, o_dm, o_dv))]
-    outs_vis = [local(n_vis.at[k], o) for k, o in enumerate((o_vp, o_vm, o_vv))]
+    go(w_xy)
+    done(w_y)
+    go(w_yx)
 
     @pl.when(is_vis)
     def _():
@@ -378,7 +413,6 @@
 
     m, v, p = adamw(gdec[...], s_dec[1], s_dec[2], s_dec[0], inv_one, inv_two)
     n_dec[0], n_dec[1], n_dec[2] = p, m, v
-    go(outs_dec)
 
     @pl.when(is_vis)
     def _():
@@ -398,41 +432,47 @@
         n_vis[0, part, :] = p
         n_vis[1, part, :] = m
         n_vis[2, part, :] = v
-    go(outs_vis)
-    done(w_y)
-
-    out_vw, out_dw = local(wall.reshape(16 * ROWS, 128), o_vw), local(dw, o_dw)
-    over_vw = remote(wall.reshape(16 * ROWS, 128), o_vw, dev(dc=1))
-    over_dw = remote(dw, o_dw, dev(dc=1))
-
-    @pl.when(is_vis)
-    def _():
-        over_vw.start()
-        out_vw.start()
-        over_dw.wait_recv()
-        out_vw.wait()
-        over_vw.wait_send()
+    done(w_xy)
+    done(w_yx)
+
+    over_v = remote(wall, w_vis, dev(dc=1))
+    over_d = remote(wall, w_dec, dev(dc=1))
+
+    @pl.when(is_vis)
+    def _():
+        over_v.start()
+        w_vis[...] = wall[...]
+        over_d.wait_recv()
+        over_v.wait_send()
         vis_over.wait_send()
 
     @pl.when(is_dec)
     def _():
-        for i in range(16):
-            wide[i * DEC : i * DEC + DEC, :] = wall[i // 4, i % 4, 0:DEC, :].astype(F32)
-
-        @pl.loop(0, DEC)
-        def _(j):
-            at = pl.multiple_of(j * 128, 128)
-            dw[:, pl.ds(at, 128)] = wide[pl.ds(j, 16, stride=DEC), :].astype(BF16)
-
-        over_dw.start()
-        out_dw.start()
-        over_vw.wait_recv()
-        out_dw.wait()
-        over_dw.wait_send()
+        over_d.start()
+        w_dec[...] = wall[...]
+        over_v.wait_recv()
+        over_d.wait_send()
         dec_over.wait_send()
 
-    done(outs_dec)
-    done(outs_vis)
+
+def finish(
+    n_dec, n_vis, w_dec, w_vis, o_dp, o_dm, o_dv, o_dw, o_vp, o_vm, o_vv, o_vw, wide, dw, sems
+):
+    pairs = [(n_dec.at[k], o) for k, o in enumerate((o_dp, o_dm, o_dv))]
+    pairs += [(n_vis.at[k], o) for k, o in enumerate((o_vp, o_vm, o_vv))]
+    pairs.append((w_vis.reshape(16 * ROWS, 128), o_vw))
+    copies = [pltpu.make_async_copy(a, b, sems.at[k]) for k, (a, b) in enumerate(pairs)]
+    for c in copies:
+        c.start()
+    for i in range(16):
+        wide[i * DEC : i * DEC + DEC, :] = w_dec[i // 4, i % 4, 0:DEC, :].astype(F32)
+    for j in range(DEC):
+        dw[:, j * 128 : j * 128 + 128] = wide[pl.ds(j, 16, stride=DEC), :].astype(BF16)
+    last = pltpu.make_async_copy(dw, o_dw, sems.at[len(pairs)])
+    last.start()
+    for c in copies:
+        c.wait()
+    last.wait()
 
 
 def body(
@@ -450,6 +490,12 @@
     anywhere = pl.BlockSpec(memory_space=pl.ANY)
     sds = jax.ShapeDtypeStruct
     vmem = pltpu.VMEM
+    inner_shape = [
+        vmem((3, DEC, 128), F32),
+        vmem((3, CAP, 128), F32),
+        vmem((4, 4, ROWS, 128), BF16),
+        vmem((4, 4, ROWS, 128), BF16),
+    ]
     out_shape = [
         sds((DEC, 128), F32),
         sds((DEC, 128), F32),
@@ -460,6 +506,7 @@
         sds((CAP, 128), F32),
         sds((16 * ROWS, 128), BF16),
     ]
+    on_chip = pl.BlockSpec(memory_space=pltpu.VMEM)
     scratch = [
         vmem((16, DEC * 128), BF16),
         vmem((16, DEC * 128), BF16),
@@ -468,9 +515,12 @@
         vmem((3, DEC, 128), F32),
         vmem((3, CAP, 128), F32),
         vmem((4, 4, ROWS, 128), F32),
-        vmem((3, 4, ROWS, 128), F32),
-        vmem((4, ROWS, 128), F32),
-        vmem((3, ROWS, 128), F32),
+        vmem((3, 4, HALF, 128), F32),
+        vmem((4, HALF, 128), F32),
+        vmem((3, 4, HALF, 128), F32),
+        vmem((4, HALF, 128), F32),
+        vmem((3, HALF, 128), F32),
+        vmem((3, HALF, 128), F32),
         vmem((PAD, 128), F32),
         vmem((3, PART, 128), F32),
         vmem((PART, 128), F32),
@@ -487,25 +537,22 @@
         vmem((16, SLOT, 128), F32),
         vmem((4, 4, SLOT, 128), F32),
         vmem((4, 4, SLOT, 128), F32),
-        vmem((3, DEC, 128), F32),
-        vmem((3, CAP, 128), F32),
-        vmem((16 * DEC, 128), F32),
-        vmem((16, DEC * 128), BF16),
+        pltpu.SMEM((16 * ROWS,), jnp.int32),
         pltpu.SemaphoreType.DMA((20,)),
         pltpu.SemaphoreType.DMA((64,)),
         pltpu.SemaphoreType.DMA((64,)),
     ]
-    outs = pl.pallas_call(
+    inner = pl.pallas_call(
         kernel,
-        out_shape=out_shape,
-        in_specs=[pl.BlockSpec(memory_space=pltpu.SMEM), pl.BlockSpec(memory_space=pltpu.VMEM)]
-        + [anywhere] * 8,
-        out_specs=[anywhere] * 8,
+        out_shape=inner_shape,
+        in_specs=[pl.BlockSpec(memory_space=pltpu.SMEM)]
+        + [pl.BlockSpec(memory_space=pltpu.HBM)] * 9,
+        out_specs=[on_chip] * 4,
         scratch_shapes=scratch,
         compiler_params=pltpu.CompilerParams(collective_id=0, has_side_effects=True),
     )(
         step_count,
-        vis_owner.reshape(16, ROWS),
+        vis_owner,
         dec_grad,
         vis_grad,
         dec_master.reshape(DEC, 128),
@@ -515,6 +562,17 @@
         vis_moment,
         vis_second,
     )
+    outs = pl.pallas_call(
+        finish,
+        out_shape=out_shape,
+        in_specs=[on_chip] * 4,
+        out_specs=[anywhere] * 8,
+        scratch_shapes=[
+            vmem((16 * DEC, 128), F32),
+            vmem((16, DEC * 128), BF16),
+            pltpu.SemaphoreType.DMA((8,)),
+        ],
+    )(*[pltpu.with_memory_space_constraint(a, pltpu.VMEM) for a in inner])
     outs = list(outs)
     for i in range(3):
         outs[i] = outs[i].reshape(1, DEC * 128)

time: 82.6 us -> 68.9 us (0.83)
  local copies, waits for them, and re-layouts: 8.49 us -> 0 us
  Pallas kernels: 72.4 us -> 67.4 us
    unnamed x20 -> x0, local copies, waits for them, and re-layouts: 7.12 us -> none
    pallas_call x1 -> x2, Pallas kernels: 72.4 us -> 67.4 us  [the longest x1 66.3 us: body(): pl.pallas_call(kernel, out_shape=inner_shape, in_specs=[pl.BlockSpec(memo...]
    reshape x1 -> x0, local copies, waits for them, and re-layouts: 1.37 us -> none  [body(): vis_owner.reshape(16, ROWS)]
where the time goes in v2:
time: 68.9 us; the launch traced here: 68.7 us
  Pallas kernels  67.4 us (98%)
  between operations  1.29 us (2%)
    pallas_call x1, Pallas kernels, body(): pl.pallas_call(kernel, out_shape=inner_shape, in_specs=[pl.BlockSpec(memo...  66.3 us

profile of v2, /device:TPU:1, one launch (start us, length us, event | category | flops | bytes accessed | tf_op | source)
XLA Modules:
  0.0 68.7 jit_solution(12597931332960270480)
XLA Ops:
  1.3 66.3 %shard_map.161 = (f32[3,64,128]{2,1,0:T(8,128)S(1)}, f32[3,160,128]{2,1,0:T(8,128)S(1)}, bf16[4,4,80,128]{3,2,1,0:T(8,128)(2,1)S(1)}, bf16[4,4,80,128]{3,2,1,0:T(8,128)(2,1)S(1)}) custom-call(s32[1]{0:T(128)S(6)} %copy.18.step_ref, s32[1280]{0:T(1024)} %own_ref.1, bf16[1,16,8192]{2,1,0:T(8,128)(2,1)} %dec_grad.1, bf16[1,1280,128]{2,1,0:T(8,128)(2,1)} %vis_grad.1, ...), custom_call_target="tpu_custom_call" | custom-call | tf_op jit(solution)/shard_map/pallas_call | solution.py:545
  67.6 1.1 %shard_map.162 = (f32[64,128]{1,0:T(8,128)}, f32[64,128]{1,0:T(8,128)}, f32[64,128]{1,0:T(8,128)}, bf16[16,8192]{1,0:T(8,128)(2,1)}, f32[160,128]{1,0:T(8,128)},...) custom-call(f32[3,64,128]{2,1,0:T(8,128)S(1)} %get-tuple-element.20.n_dec, ...), custom_call_target="tpu_custom_call" | custom-call | tf_op jit(solution)/shard_map/pallas_call | solution.py:565

commit v3 on v2

--- a/solution.py
+++ b/solution.py
@@ -52,8 +52,8 @@
     vis_v,
     n_dec,
     n_vis,
-    w_dec,
-    w_vis,
+    wall,
+    other,
     a_dec,
     b_dec,
     a_vis,
@@ -76,7 +76,6 @@
     tz,
     g4,
     gdec,
-    wall,
     st,
     stm,
     stx,
@@ -87,6 +86,8 @@
     lsem,
     ssem,
     rsem,
+    near_sem,
+    far_sem,
 ):
     rep, sh = lax.axis_index("replica"), lax.axis_index("shard")
     core = lax.rem(rep, 2)
@@ -165,12 +166,15 @@
 
     friends = [dev(dc=1)]
     friends += [dev(dx=d) for d in (1, -1, 2)]
-    friends += [dev(dy=d) for d in (1, -1, 2, -2, 4)]
-    friends += [dev(dz=d) for d in (1, -1, 2, -2, 4, -4, 8)]
+    friends += [dev(dy=d) for d in (1, -1, 2, -2)]
+    friends += [dev(dz=d) for d in (1, -1, 2, -2)]
     barrier = pltpu.get_barrier_semaphore()
     for friend in friends:
         pl.semaphore_signal(barrier, inc=1, device_id=friend, device_id_type=MESH)
     pl.semaphore_wait(barrier, len(friends))
+
+    for d in (2, -2):
+        pl.semaphore_signal(near_sem, inc=1, device_id=dev(dz=d), device_id_type=MESH)
 
     send_vis = remote(vis_grad.at[0], b_vis, dev(dc=1))
     send_dec = remote(dec_grad.at[0], b_dec, dev(dc=1))
@@ -231,6 +235,9 @@
         remote(ak.at[q1], ry2.at[0], dev(dy=1)),
         remote(ak.at[q3], ry2.at[1], dev(dy=-1)),
     ]
+    pl.semaphore_wait(near_sem, 2)
+    for d in (4, -4):
+        pl.semaphore_signal(far_sem, inc=1, device_id=dev(dz=d), device_id_type=MESH)
     done(first_y)
     for i in range(NX):
         ay[i] = (acc[i, yl, one, :] + ry[0, i]) + (ry[1, i] + ry[2, i])
@@ -275,7 +282,6 @@
 
     st_x = along_x(st, stm)
     st_y = along_y(stm, stx)
-    back = [at4(x, d) for d in (-2, -1, 1)]
 
     @pl.when(is_vis)
     def _():
@@ -285,26 +291,42 @@
     done(copies)
     az[...] = (ax[part_of(zq), :] + rz[0]) + (rz[1] + rz[2])
 
-    far = remote(az, ryh, dev(dy=4))
-    far.start()
+    ra, rb = pl.ds(0, 16), pl.ds(16, PART - 16)
+
+    def along_far_z(src, rows):
+        return [
+            remote(src.at[rows], rzh.at[2, rows], dev(dz=8)),
+            remote(src.at[rows], rzh.at[0, rows], dev(dz=4)),
+            remote(src.at[rows], rzh.at[1, rows], dev(dz=-4)),
+        ]
+
+    def far_sum(own, rows):
+        return (own[rows, :] + rzh[2, rows, :]) + (rzh[0, rows, :] + rzh[1, rows, :])
+
+    far_a = remote(az.at[ra], ryh.at[ra], dev(dy=4))
+    far_a.start()
+    pl.semaphore_wait(far_sem, 2)
+    z_b = along_far_z(az, rb)
+    go(z_b)
 
     @pl.when(is_vis)
     def _():
         done(st_x)
 
-    far.wait()
-    ah[...] = az[...] + ryh[...]
-    copies = [
-        remote(ah, rzh.at[2], dev(dz=8)),
-        remote(ah, rzh.at[0], dev(dz=4)),
-        remote(ah, rzh.at[1], dev(dz=-4)),
-    ]
-    go(copies)
+    far_a.wait()
+    ah[ra, :] = az[ra, :] + ryh[ra, :]
+    z_a = along_far_z(ah, ra)
+    go(z_a)
 
     @pl.when(is_vis)
     def _():
         go(st_y)
         stx[:, yl] = stm[:, yl]
+
+    done(z_b)
+    ah[rb, :] = far_sum(az, rb)
+    far_b = remote(ah.at[rb], ryh.at[rb], dev(dy=4))
+    far_b.start()
 
     done(load_maps)
     t = jnp.full((1, 128), step_ref[0].astype(F32), F32)
@@ -340,8 +362,10 @@
         for k in range(3):
             n_vis[k, 0:ROWS, :] = blocks_of(k)
 
-    done(copies)
-    tz[...] = (ah[...] + rzh[2]) + (rzh[0] + rzh[1])
+    far_b.wait()
+    tz[rb, :] = ah[rb, :] + ryh[rb, :]
+    done(z_a)
+    tz[ra, :] = far_sum(ah, ra)
 
     copies = [
         remote(tz, g4.at[zq], dev(dz=2)),
@@ -393,16 +417,25 @@
         gm[x] = gx[pl.ds(x * 4, 4)]
 
     w_xy = [
+        weights(wall.at[:, yl, up], dev(dy=1)),
+        weights(wall.at[:, yl, up], dev(dy=-1)),
         weights(wall.at[lo, yl, up], dev(dy=2)),
         weights(wall.at[hi, yl, up], dev(dy=-2)),
-        weights(wall.at[:, yl, up], dev(dy=1)),
-        weights(wall.at[:, yl, up], dev(dy=-1)),
-    ]
-    w_yx = [weights(wall.at[x, :, down], dev(dx=d)) for d in (2, 1, -1)]
+    ]
+    w_yx = [weights(wall.at[x, :, down], dev(dx=d)) for d in (1, -1, 2)]
+    over = []
+
+    def forward(*index):
+        over.append(remote(wall.at[index], other.at[index], dev(dc=1)))
+        over[-1].start()
+
+    every = pl.ds(0, 4)
     done(w_x)
     go(w_xy)
+    forward(every, yl, up)
     done(w_y)
     go(w_yx)
+    forward(x, every, down)
 
     @pl.when(is_vis)
     def _():
@@ -418,6 +451,21 @@
     def _():
         done(g_y)
         vis_over.start()
+
+    w_xy[0].wait()
+    forward(every, q3, up)
+    w_yx[0].wait()
+    forward(x3, every, down)
+    w_xy[1].wait()
+    forward(every, q1, up)
+    w_yx[1].wait()
+    forward(x1, every, down)
+    w_xy[2].wait()
+    forward(lo, q2, up)
+    w_xy[3].wait()
+    forward(hi, q2, up)
+    w_yx[2].wait()
+    forward(x2, every, down)
 
     @pl.when(is_dec)
     def _():
@@ -432,47 +480,49 @@
         n_vis[0, part, :] = p
         n_vis[1, part, :] = m
         n_vis[2, part, :] = v
-    done(w_xy)
-    done(w_yx)
-
-    over_v = remote(wall, w_vis, dev(dc=1))
-    over_d = remote(wall, w_dec, dev(dc=1))
-
-    @pl.when(is_vis)
-    def _():
-        over_v.start()
-        w_vis[...] = wall[...]
-        over_d.wait_recv()
-        over_v.wait_send()
+    done(over)
+
+    @pl.when(is_vis)
+    def _():
         vis_over.wait_send()
 
     @pl.when(is_dec)
     def _():
-        over_d.start()
-        w_dec[...] = wall[...]
-        over_v.wait_recv()
-        over_d.wait_send()
         dec_over.wait_send()
 
 
 def finish(
-    n_dec, n_vis, w_dec, w_vis, o_dp, o_dm, o_dv, o_dw, o_vp, o_vm, o_vv, o_vw, wide, dw, sems
+    n_dec, n_vis, mine, other, o_dp, o_dm, o_dv, o_dw, o_vp, o_vm, o_vv, o_vw, wide, dw, sems
 ):
+    core = lax.rem(lax.axis_index("replica"), 2)
     pairs = [(n_dec.at[k], o) for k, o in enumerate((o_dp, o_dm, o_dv))]
     pairs += [(n_vis.at[k], o) for k, o in enumerate((o_vp, o_vm, o_vv))]
-    pairs.append((w_vis.reshape(16 * ROWS, 128), o_vw))
     copies = [pltpu.make_async_copy(a, b, sems.at[k]) for k, (a, b) in enumerate(pairs)]
     for c in copies:
         c.start()
-    for i in range(16):
-        wide[i * DEC : i * DEC + DEC, :] = w_dec[i // 4, i % 4, 0:DEC, :].astype(F32)
-    for j in range(DEC):
-        dw[:, j * 128 : j * 128 + 128] = wide[pl.ds(j, 16, stride=DEC), :].astype(BF16)
-    last = pltpu.make_async_copy(dw, o_dw, sems.at[len(pairs)])
-    last.start()
+
+    def weights(dec, vis):
+        first = pltpu.make_async_copy(vis.reshape(16 * ROWS, 128), o_vw, sems.at[len(pairs)])
+        first.start()
+        for i in range(16):
+            wide[i * DEC : i * DEC + DEC, :] = dec[i // 4, i % 4, 0:DEC, :].astype(F32)
+        for j in range(DEC):
+            dw[:, j * 128 : j * 128 + 128] = wide[pl.ds(j, 16, stride=DEC), :].astype(BF16)
+        last = pltpu.make_async_copy(dw, o_dw, sems.at[len(pairs) + 1])
+        last.start()
+        first.wait()
+        last.wait()
+
+    @pl.when(core == 0)
+    def _():
+        weights(mine, other)
+
+    @pl.when(core == 1)
+    def _():
+        weights(other, mine)
+
     for c in copies:
         c.wait()
-    last.wait()
 
 
 def body(
@@ -530,7 +580,6 @@
         vmem((PART, 128), F32),
         vmem((4, PART, 128), F32),
         vmem((DEC, 128), F32),
-        vmem((4, 4, ROWS, 128), BF16),
         vmem((16, 3 * SLOT, 128), F32),
         vmem((4, 4, 3 * SLOT, 128), F32),
         vmem((4, 4, 3 * SLOT, 128), F32),
@@ -539,8 +588,10 @@
         vmem((4, 4, SLOT, 128), F32),
         pltpu.SMEM((16 * ROWS,), jnp.int32),
         pltpu.SemaphoreType.DMA((20,)),
-        pltpu.SemaphoreType.DMA((64,)),
-        pltpu.SemaphoreType.DMA((64,)),
+        pltpu.SemaphoreType.DMA((96,)),
+        pltpu.SemaphoreType.DMA((96,)),
+        pltpu.SemaphoreType.REGULAR,
+        pltpu.SemaphoreType.REGULAR,
     ]
     inner = pl.pallas_call(
         kernel,

time: 68.9 us -> 63.6 us (0.923)
  Pallas kernels: 67.4 us -> 62.1 us
    pallas_call x1, Pallas kernels: 66.3 us -> 61 us  [body(): pl.pallas_call(kernel, out_shape=inner_shape, in_specs=[pl.BlockSpec(memo...]
where the time goes in v3:
time: 63.6 us; the launch traced here: 63.4 us
  Pallas kernels  62.1 us (98%)
  between operations  1.29 us (2%)
    pallas_call x1, Pallas kernels, body(): pl.pallas_call(kernel, out_shape=inner_shape, in_specs=[pl.BlockSpec(memo...  61 us

profile of v3, /device:TPU:1, one launch (start us, length us, event | category | flops | bytes accessed | tf_op | source)
XLA Modules:
  0.0 63.4 jit_solution(15579377113085844402)
XLA Ops:
  1.3 61.0 %shard_map.161 = (f32[3,64,128]{2,1,0:T(8,128)S(1)}, f32[3,160,128]{2,1,0:T(8,128)S(1)}, bf16[4,4,80,128]{3,2,1,0:T(8,128)(2,1)S(1)}, bf16[4,4,80,128]{3,2,1,0:T(8,128)(2,1)S(1)}) custom-call(s32[1]{0:T(128)S(6)} %copy.18.step_ref, s32[1280]{0:T(1024)} %own_ref.1, bf16[1,16,8192]{2,1,0:T(8,128)(2,1)} %dec_grad.1, bf16[1,1280,128]{2,1,0:T(8,128)(2,1)} %vis_grad.1, ...), custom_call_target="tpu_custom_call" | custom-call | tf_op jit(solution)/shard_map/pallas_call | solution.py:596
  62.3 1.1 %shard_map.162 = (f32[64,128]{1,0:T(8,128)}, f32[64,128]{1,0:T(8,128)}, f32[64,128]{1,0:T(8,128)}, bf16[16,8192]{1,0:T(8,128)(2,1)}, f32[160,128]{1,0:T(8,128)},...) custom-call(f32[3,64,128]{2,1,0:T(8,128)S(1)} %get-tuple-element.20.n_dec, ...), custom_call_target="tpu_custom_call" | custom-call | tf_op jit(solution)/shard_map/pallas_call | solution.py:616

commit v4 on v3

--- a/solution.py
+++ b/solution.py
@@ -30,6 +30,8 @@
 SLOT = 16
 USED = 10
 CAP = 160
+LOCALS, REMOTES = 9, 65
+SENDS = 24
 
 
 def adamw(g, m, v, p, inv_one, inv_two):
@@ -83,6 +85,7 @@
     gm,
     gr,
     owner,
+    pick,
     lsem,
     ssem,
     rsem,
@@ -115,7 +118,7 @@
         return pltpu.make_async_remote_copy(
             src_ref=src,
             dst_ref=dst,
-            send_sem=ssem.at[k],
+            send_sem=ssem.at[k % SENDS],
             recv_sem=rsem.at[k],
             device_id=target,
             device_id_type=MESH,
@@ -191,8 +194,6 @@
             block = a_dec[:, pl.ds(at, 128)].astype(F32) + b_dec[:, pl.ds(at, 128)].astype(F32)
             acc.reshape(16 * ROWS, 128)[pl.ds(j, 16, stride=ROWS), :] = block
 
-        for i in range(16):
-            acc[i // 4, i % 4, DEC:ROWS, :] = jnp.zeros((ROWS - DEC, 128), F32)
         send_vis.wait_send()
 
     @pl.when(is_vis)
@@ -206,51 +207,99 @@
             acc[i // 4, i % 4] = a_vis[part, :].astype(F32) + b_vis[part, :].astype(F32)
         send_dec.wait_send()
 
+    def prepare():
+        done(load_state)
+        done(load_maps)
+        for i in range(16):
+            for k in range(3):
+                st[i, k * SLOT : k * SLOT + SLOT, :] = jnp.zeros((SLOT, 128), F32)
+                st[i, k * SLOT : k * SLOT + USED, :] = s_vis[k, i * USED : i * USED + USED, :]
+        lane = lax.broadcasted_iota(jnp.int32, (1, ROWS), 1)
+        own = lax.fori_loop(
+            0,
+            ROWS,
+            lambda i, v: jnp.where(lane == i, owner[sh * ROWS + i], v),
+            jnp.zeros((1, ROWS), jnp.int32),
+        )
+        one_hot = (lax.broadcasted_iota(jnp.int32, (16, ROWS), 0) == own).astype(F32)
+        before = (
+            lax.broadcasted_iota(jnp.int32, (ROWS, ROWS), 0)
+            < lax.broadcasted_iota(jnp.int32, (ROWS, ROWS), 1)
+        ).astype(F32)
+        count = jnp.dot(one_hot, before, preferred_element_type=F32)
+        position = jnp.sum(one_hot * count, axis=0, keepdims=True)
+        key = own * SLOT + position.astype(jnp.int32)
+        pick[...] = (lax.broadcasted_iota(jnp.int32, (16 * SLOT, ROWS), 0) == key).astype(F32)
+
     q1, q2, q3 = at4(yl, 1), at4(yl, 2), at4(yl, 3)
     x1, x2, x3 = at4(x, 1), at4(x, 2), at4(x, 3)
     lo, hi = pl.ds(0, 2), pl.ds(2, 2)
-    one, two = pl.ds(0, HALF), pl.ds(HALF, HALF)
-    first_y = [
-        remote(acc.at[lo, q2, one], ry.at[2, lo], dev(dy=2)),
-        remote(acc.at[hi, q2, one], ry.at[2, hi], dev(dy=-2)),
-        remote(acc.at[:, q1, one], ry.at[0], dev(dy=1)),
-        remote(acc.at[:, q3, one], ry.at[1], dev(dy=-1)),
-    ]
-    first_x = [
-        remote(acc.at[x2, :, two], rx.at[2], dev(dx=2)),
-        remote(acc.at[x1, :, two], rx.at[0], dev(dx=1)),
-        remote(acc.at[x3, :, two], rx.at[1], dev(dx=-1)),
-    ]
-    for a, b in itertools.zip_longest(first_y, first_x):
-        a.start()
-        if b is not None:
-            b.start()
-    second_x = [
-        remote(ay.at[x2], rx2.at[2], dev(dx=2)),
-        remote(ay.at[x1], rx2.at[0], dev(dx=1)),
-        remote(ay.at[x3], rx2.at[1], dev(dx=-1)),
-    ]
-    second_y = [
-        remote(ak.at[q2], ry2.at[2], dev(dy=2)),
-        remote(ak.at[q1], ry2.at[0], dev(dy=1)),
-        remote(ak.at[q3], ry2.at[1], dev(dy=-1)),
-    ]
-    pl.semaphore_wait(near_sem, 2)
-    for d in (4, -4):
-        pl.semaphore_signal(far_sem, inc=1, device_id=dev(dz=d), device_id_type=MESH)
-    done(first_y)
-    for i in range(NX):
-        ay[i] = (acc[i, yl, one, :] + ry[0, i]) + (ry[1, i] + ry[2, i])
-    go(second_x)
-    done(first_x)
-    for i in range(Q):
-        ak[i] = (acc[x, i, two, :] + rx[0, i]) + (rx[1, i] + rx[2, i])
-    go(second_y)
-    done(second_x)
-    ax[0:HALF, :] = (ay[x] + rx2[0]) + (rx2[1] + rx2[2])
-    done(second_y)
-    ax[HALF:ROWS, :] = (ak[yl] + ry2[0]) + (ry2[1] + ry2[2])
-    ax[ROWS:PAD, :] = jnp.zeros((PAD - ROWS, 128), F32)
+
+    def scatter(rows):
+        half = rows // 2
+        one, two, part = pl.ds(0, half), pl.ds(half, half), pl.ds(0, half)
+        first_y = [
+            remote(acc.at[lo, q2, one], ry.at[2, lo, part], dev(dy=2)),
+            remote(acc.at[hi, q2, one], ry.at[2, hi, part], dev(dy=-2)),
+            remote(acc.at[:, q1, one], ry.at[0, :, part], dev(dy=1)),
+            remote(acc.at[:, q3, one], ry.at[1, :, part], dev(dy=-1)),
+        ]
+        first_x = [
+            remote(acc.at[x2, :, two], rx.at[2, :, part], dev(dx=2)),
+            remote(acc.at[x1, :, two], rx.at[0, :, part], dev(dx=1)),
+            remote(acc.at[x3, :, two], rx.at[1, :, part], dev(dx=-1)),
+        ]
+        second_x = [
+            remote(ay.at[x2, part], rx2.at[2, part], dev(dx=2)),
+            remote(ay.at[x1, part], rx2.at[0, part], dev(dx=1)),
+            remote(ay.at[x3, part], rx2.at[1, part], dev(dx=-1)),
+        ]
+        second_y = [
+            remote(ak.at[q2, part], ry2.at[2, part], dev(dy=2)),
+            remote(ak.at[q1, part], ry2.at[0, part], dev(dy=1)),
+            remote(ak.at[q3, part], ry2.at[1, part], dev(dy=-1)),
+        ]
+        for a, b in itertools.zip_longest(first_y, first_x):
+            a.start()
+            if b is not None:
+                b.start()
+        pl.semaphore_wait(near_sem, 2)
+        for d in (4, -4):
+            pl.semaphore_signal(far_sem, inc=1, device_id=dev(dz=d), device_id_type=MESH)
+        if rows == ROWS:
+            prepare()
+        else:
+            done(load_state)
+            done(load_maps)
+        done(first_y)
+        for i in range(NX):
+            ay[i, part, :] = (acc[i, yl, one, :] + ry[0, i, part, :]) + (
+                ry[1, i, part, :] + ry[2, i, part, :]
+            )
+        go(second_x)
+        done(first_x)
+        for i in range(Q):
+            ak[i, part, :] = (acc[x, i, two, :] + rx[0, i, part, :]) + (
+                rx[1, i, part, :] + rx[2, i, part, :]
+            )
+        go(second_y)
+        done(second_x)
+        ax[one, :] = (ay[x, part, :] + rx2[0, part, :]) + (rx2[1, part, :] + rx2[2, part, :])
+        done(second_y)
+        ax[two, :] = (ak[yl, part, :] + ry2[0, part, :]) + (ry2[1, part, :] + ry2[2, part, :])
+        ax[rows:PAD, :] = jnp.zeros((PAD - rows, 128), F32)
+
+    mark = used[0]
+
+    @pl.when(is_dec)
+    def _():
+        scatter(DEC)
+
+    used[0] = mark
+
+    @pl.when(is_vis)
+    def _():
+        scatter(ROWS)
 
     def part_of(i):
         return pl.ds(pl.multiple_of(i * PART, 8), PART)
@@ -262,12 +311,6 @@
     ]
     go(copies)
 
-    done(load_state)
-    for i in range(16):
-        for k in range(3):
-            st[i, k * SLOT : k * SLOT + SLOT, :] = jnp.zeros((SLOT, 128), F32)
-            st[i, k * SLOT : k * SLOT + USED, :] = s_vis[k, i * USED : i * USED + USED, :]
-
     def along_x(src, dst):
         return [
             remote(src.at[pl.ds(at4(x, d) * 4, 4)], dst.at[x], dev(dx=e))
@@ -328,32 +371,14 @@
     far_b = remote(ah.at[rb], ryh.at[rb], dev(dy=4))
     far_b.start()
 
-    done(load_maps)
     t = jnp.full((1, 128), step_ref[0].astype(F32), F32)
     inv_one = 1.0 / (1.0 - jnp.exp(t * math.log(beta_one)))
     inv_two = 1.0 / (1.0 - jnp.exp(t * math.log(beta_two)))
 
-    lane = lax.broadcasted_iota(jnp.int32, (1, ROWS), 1)
-    own = lax.fori_loop(
-        0,
-        ROWS,
-        lambda i, v: jnp.where(lane == i, owner[sh * ROWS + i], v),
-        jnp.zeros((1, ROWS), jnp.int32),
-    )
-    one_hot = (lax.broadcasted_iota(jnp.int32, (16, ROWS), 0) == own).astype(F32)
-    before = (
-        lax.broadcasted_iota(jnp.int32, (ROWS, ROWS), 0)
-        < lax.broadcasted_iota(jnp.int32, (ROWS, ROWS), 1)
-    ).astype(F32)
-    count = jnp.dot(one_hot, before, preferred_element_type=F32)
-    position = jnp.sum(one_hot * count, axis=0, keepdims=True)
-    key = own * SLOT + position.astype(jnp.int32)
-    pick = (lax.broadcasted_iota(jnp.int32, (16 * SLOT, ROWS), 0) == key).astype(F32)
-
     def blocks_of(k):
         rows = stx[:, :, k * SLOT : k * SLOT + SLOT, :].reshape(16 * SLOT, 128)
         return lax.dot_general(
-            pick, rows, (((0,), (0,)), ((), ())), precision=HIGH, preferred_element_type=F32
+            pick[...], rows, (((0,), (0,)), ((), ())), precision=HIGH, preferred_element_type=F32
         )
 
     @pl.when(is_vis)
@@ -381,114 +406,114 @@
     dec_over = remote(gdec, gdec, dev(dc=1))
     vis_over = remote(gr, gr, dev(dc=1))
 
+    class Gather:
+        def __init__(self, rows, top):
+            up, down = pl.ds(0, top), pl.ds(top, rows - top)
+            every = pl.ds(0, 4)
+
+            def same(view, device):
+                return remote(view, view, device)
+
+            self.x = [same(wall.at[x, yl, up], dev(dx=d)) for d in (2, 1, -1)]
+            self.y = [same(wall.at[x, yl, down], dev(dy=d)) for d in (2, 1, -1)]
+            self.xy = [
+                same(wall.at[:, yl, up], dev(dy=1)),
+                same(wall.at[:, yl, up], dev(dy=-1)),
+                same(wall.at[lo, yl, up], dev(dy=2)),
+                same(wall.at[hi, yl, up], dev(dy=-2)),
+            ]
+            self.yx = [same(wall.at[x, :, down], dev(dx=d)) for d in (1, -1, 2)]
+            self.over = [
+                remote(wall.at[index], other.at[index], dev(dc=1))
+                for index in (
+                    (every, yl, up),
+                    (x, every, down),
+                    (every, q3, up),
+                    (x3, every, down),
+                    (every, q1, up),
+                    (x1, every, down),
+                    (lo, q2, up),
+                    (hi, q2, up),
+                    (x2, every, down),
+                )
+            ]
+
+    mark = used[0]
+    of_dec = Gather(DEC, 32)
+    used[0] = mark
+    of_vis = Gather(ROWS, CUT)
+
+    def tail(rows, vision):
+        mine, theirs = (of_vis, of_dec) if vision else (of_dec, of_vis)
+        g = g4[...].reshape(PAD, 128)[0:rows]
+        if vision:
+            m, v, p = n_vis[1, 0:rows, :], n_vis[2, 0:rows, :], n_vis[0, 0:rows, :]
+        else:
+            gdec[...] = g
+            dec_over.start()
+            m, v, p = s_dec[1], s_dec[2], s_dec[0]
+        wall[x, yl, 0:rows, :] = adamw(g, m, v, p, inv_one, inv_two)[2].astype(BF16)
+        go(mine.x)
+        go(mine.y)
+        if vision:
+            gx[...] = jnp.dot(pick[...], g, precision=HIGH, preferred_element_type=F32).reshape(
+                16, SLOT, 128
+            )
+            go(g_x)
+            gm[x] = gx[pl.ds(x * 4, 4)]
+        done(mine.x)
+        go(mine.xy)
+        mine.over[0].start()
+        done(mine.y)
+        go(mine.yx)
+        mine.over[1].start()
+        if vision:
+            done(g_x)
+            go(g_y)
+            gr[:, yl] = gm[:, yl]
+            dec_over.wait_recv()
+        m, v, p = adamw(gdec[...], s_dec[1], s_dec[2], s_dec[0], inv_one, inv_two)
+        n_dec[0], n_dec[1], n_dec[2] = p, m, v
+        if vision:
+            done(g_y)
+            vis_over.start()
+        arrivals = (mine.xy[0], mine.yx[0], mine.xy[1], mine.yx[1], mine.xy[2], mine.xy[3], mine.yx[2])
+        for a, b in zip(arrivals, mine.over[2:]):
+            a.wait()
+            b.start()
+        if not vision:
+            vis_over.wait_recv()
+        for i in range(16):
+            part = pl.ds(i * USED, USED)
+            m, v, p = adamw(
+                gr[i // 4, i % 4, 0:USED, :],
+                s_vis[1, part, :],
+                s_vis[2, part, :],
+                s_vis[0, part, :],
+                inv_one,
+                inv_two,
+            )
+            n_vis[0, part, :] = p
+            n_vis[1, part, :] = m
+            n_vis[2, part, :] = v
+        for c in mine.over:
+            c.wait_send()
+        for c in theirs.over:
+            c.wait_recv()
+        if vision:
+            vis_over.wait_send()
+        else:
+            dec_over.wait_send()
+
     @pl.when(is_dec)
     def _():
-        g = g4[...].reshape(PAD, 128)[0:DEC]
-        gdec[...] = g
-        dec_over.start()
-        _, _, p = adamw(g, s_dec[1], s_dec[2], s_dec[0], inv_one, inv_two)
-        wall[x, yl, 0:DEC, :] = p.astype(BF16)
-        wall[x, yl, DEC:ROWS, :] = jnp.zeros((ROWS - DEC, 128), BF16)
-
-    @pl.when(is_vis)
-    def _():
-        g = g4[...].reshape(PAD, 128)[0:ROWS]
-        _, _, p = adamw(
-            g, n_vis[1, 0:ROWS, :], n_vis[2, 0:ROWS, :], n_vis[0, 0:ROWS, :], inv_one, inv_two
-        )
-        wall[x, yl] = p.astype(BF16)
-
-    up, down = pl.ds(0, CUT), pl.ds(CUT, ROWS - CUT)
-
-    def weights(view, device):
-        return remote(view, view, device)
-
-    w_x = [weights(wall.at[x, yl, up], dev(dx=d)) for d in (2, 1, -1)]
-    w_y = [weights(wall.at[x, yl, down], dev(dy=d)) for d in (2, 1, -1)]
-    go(w_x)
-    go(w_y)
-
-    @pl.when(is_vis)
-    def _():
-        g = g4[...].reshape(PAD, 128)[0:ROWS]
-        rows = jnp.dot(pick, g, precision=HIGH, preferred_element_type=F32)
-        gx[...] = rows.reshape(16, SLOT, 128)
-        go(g_x)
-        gm[x] = gx[pl.ds(x * 4, 4)]
-
-    w_xy = [
-        weights(wall.at[:, yl, up], dev(dy=1)),
-        weights(wall.at[:, yl, up], dev(dy=-1)),
-        weights(wall.at[lo, yl, up], dev(dy=2)),
-        weights(wall.at[hi, yl, up], dev(dy=-2)),
-    ]
-    w_yx = [weights(wall.at[x, :, down], dev(dx=d)) for d in (1, -1, 2)]
-    over = []
-
-    def forward(*index):
-        over.append(remote(wall.at[index], other.at[index], dev(dc=1)))
-        over[-1].start()
-
-    every = pl.ds(0, 4)
-    done(w_x)
-    go(w_xy)
-    forward(every, yl, up)
-    done(w_y)
-    go(w_yx)
-    forward(x, every, down)
-
-    @pl.when(is_vis)
-    def _():
-        done(g_x)
-        go(g_y)
-        gr[:, yl] = gm[:, yl]
-        dec_over.wait_recv()
-
-    m, v, p = adamw(gdec[...], s_dec[1], s_dec[2], s_dec[0], inv_one, inv_two)
-    n_dec[0], n_dec[1], n_dec[2] = p, m, v
-
-    @pl.when(is_vis)
-    def _():
-        done(g_y)
-        vis_over.start()
-
-    w_xy[0].wait()
-    forward(every, q3, up)
-    w_yx[0].wait()
-    forward(x3, every, down)
-    w_xy[1].wait()
-    forward(every, q1, up)
-    w_yx[1].wait()
-    forward(x1, every, down)
-    w_xy[2].wait()
-    forward(lo, q2, up)
-    w_xy[3].wait()
-    forward(hi, q2, up)
-    w_yx[2].wait()
-    forward(x2, every, down)
-
-    @pl.when(is_dec)
-    def _():
-        vis_over.wait_recv()
-
-    for i in range(16):
-        part = pl.ds(i * USED, USED)
-        g = gr[i // 4, i % 4, 0:USED, :]
-        m, v, p = adamw(
-            g, s_vis[1, part, :], s_vis[2, part, :], s_vis[0, part, :], inv_one, inv_two
-        )
-        n_vis[0, part, :] = p
-        n_vis[1, part, :] = m
-        n_vis[2, part, :] = v
-    done(over)
-
-    @pl.when(is_vis)
-    def _():
-        vis_over.wait_send()
-
-    @pl.when(is_dec)
-    def _():
-        dec_over.wait_send()
+        tail(DEC, False)
+
+    @pl.when(is_vis)
+    def _():
+        tail(ROWS, True)
+
+    assert (locals_used[0], used[0]) == (LOCALS, REMOTES), (locals_used, used)
 
 
 def finish(
@@ -587,9 +612,10 @@
         vmem((4, 4, SLOT, 128), F32),
         vmem((4, 4, SLOT, 128), F32),
         pltpu.SMEM((16 * ROWS,), jnp.int32),
-        pltpu.SemaphoreType.DMA((20,)),
-        pltpu.SemaphoreType.DMA((96,)),
-        pltpu.SemaphoreType.DMA((96,)),
+        vmem((16 * SLOT, ROWS), F32),
+        pltpu.SemaphoreType.DMA((LOCALS,)),
+        pltpu.SemaphoreType.DMA((SENDS,)),
+        pltpu.SemaphoreType.DMA((REMOTES,)),
         pltpu.SemaphoreType.REGULAR,
         pltpu.SemaphoreType.REGULAR,
     ]

time: 63.6 us -> 62.1 us (0.976)
  Pallas kernels: 62.1 us -> 60.6 us
    pallas_call x1, Pallas kernels: 61 us -> 59.5 us  [body(): pl.pallas_call(kernel, out_shape=inner_shape, in_specs=[pl.BlockSpec(memo...]
where the time goes in v4:
time: 62.1 us; the launch traced here: 61.9 us
  Pallas kernels  60.6 us (98%)
  between operations  1.29 us (2%)
    pallas_call x1, Pallas kernels, body(): pl.pallas_call(kernel, out_shape=inner_shape, in_specs=[pl.BlockSpec(memo...  59.5 us

profile of v4, /device:TPU:1, one launch (start us, length us, event | category | flops | bytes accessed | tf_op | source)
XLA Modules:
  0.0 61.9 jit_solution(3689831084844937338)
XLA Ops:
  1.3 59.5 %shard_map.161 = (f32[3,64,128]{2,1,0:T(8,128)S(1)}, f32[3,160,128]{2,1,0:T(8,128)S(1)}, bf16[4,4,80,128]{3,2,1,0:T(8,128)(2,1)S(1)}, bf16[4,4,80,128]{3,2,1,0:T(8,128)(2,1)S(1)}) custom-call(s32[1]{0:T(128)S(6)} %copy.18.step_ref, s32[1280]{0:T(1024)} %own_ref.1, bf16[1,16,8192]{2,1,0:T(8,128)(2,1)} %dec_grad.1, bf16[1,1280,128]{2,1,0:T(8,128)(2,1)} %vis_grad.1, ...), custom_call_target="tpu_custom_call" | custom-call | tf_op jit(solution)/shard_map/pallas_call | solution.py:622
  60.8 1.1 %shard_map.162 = (f32[64,128]{1,0:T(8,128)}, f32[64,128]{1,0:T(8,128)}, f32[64,128]{1,0:T(8,128)}, bf16[16,8192]{1,0:T(8,128)(2,1)}, f32[160,128]{1,0:T(8,128)},...) custom-call(f32[3,64,128]{2,1,0:T(8,128)S(1)} %get-tuple-element.20.n_dec, ...), custom_call_target="tpu_custom_call" | custom-call | tf_op jit(solution)/shard_map/pallas_call | solution.py:642

commit v5 on v4

--- a/solution.py
+++ b/solution.py
@@ -25,7 +25,7 @@
 DEC = 64
 PAD = 96
 HALF = ROWS // 2
-CUT = 48
+CUT = 40
 PART = PAD // 4
 SLOT = 16
 USED = 10

time: 62.1 us -> 62.1 us (level)
  no operation moved by 1% of the time
where the time goes in v5:
time: 62.1 us; the launch traced here: 61.9 us
  Pallas kernels  60.6 us (98%)
  between operations  1.29 us (2%)
    pallas_call x1, Pallas kernels, body(): pl.pallas_call(kernel, out_shape=inner_shape, in_specs=[pl.BlockSpec(memo...  59.5 us

profile of v5, /device:TPU:1, one launch (start us, length us, event | category | flops | bytes accessed | tf_op | source)
XLA Modules:
  0.0 61.9 jit_solution(17906588234181672740)
XLA Ops:
  1.3 59.5 %shard_map.161 = (f32[3,64,128]{2,1,0:T(8,128)S(1)}, f32[3,160,128]{2,1,0:T(8,128)S(1)}, bf16[4,4,80,128]{3,2,1,0:T(8,128)(2,1)S(1)}, bf16[4,4,80,128]{3,2,1,0:T(8,128)(2,1)S(1)}) custom-call(s32[1]{0:T(128)S(6)} %copy.18.step_ref, s32[1280]{0:T(1024)} %own_ref.1, bf16[1,16,8192]{2,1,0:T(8,128)(2,1)} %dec_grad.1, bf16[1,1280,128]{2,1,0:T(8,128)(2,1)} %vis_grad.1, ...), custom_call_target="tpu_custom_call" | custom-call | tf_op jit(solution)/shard_map/pallas_call | solution.py:622
  60.8 1.1 %shard_map.162 = (f32[64,128]{1,0:T(8,128)}, f32[64,128]{1,0:T(8,128)}, f32[64,128]{1,0:T(8,128)}, bf16[16,8192]{1,0:T(8,128)(2,1)}, f32[160,128]{1,0:T(8,128)},...) custom-call(f32[3,64,128]{2,1,0:T(8,128)S(1)} %get-tuple-element.20.n_dec, ...), custom_call_target="tpu_custom_call" | custom-call | tf_op jit(solution)/shard_map/pallas_call | solution.py:642
